TPU v7x, 32 devices: a whole 2x2x4 slice. The times are simulated.
32 devices in a mesh: groups: 2 (over y), seq: 8 (over z, core), section: 2 (over x), tp: 1.
Axes of the slice: x: 2, y: 2, z: 4, core: 2. Of those that a mesh axis runs over, the one named last changes fastest.
Arguments:
- stream: bfloat16 [4, 512, 1536], P('groups', 'seq', 'tp'), parts along dimension 0, may hold values from -30 to 30
- set_views: int32 [4, 6], P('groups'), parts along dimension 0, may hold values from 1 to 2, 8 in all within a row
- modulation: bfloat16 [2, 4, 6, 2, 1536], P('section', 'groups', None, None, 'tp'), parts along dimension 1, may hold values from -2.5 to 2.5
- set_gate: bfloat16 [2, 4, 6, 1536], P('section', 'groups', None, 'tp'), parts along dimension 1, may hold values from 0.5 to 1.5
- qkv_weight: bfloat16 [2, 1536, 3, 1536], P('section', 'seq', None, 'tp'), may hold values from -0.15625 to 0.15625
- norm_gain: float32 [2, 2, 128], P('section'), may hold values from 0.1 to 1.9
- out_weight: bfloat16 [2, 1536, 1536], P('section', None, 'tp'), may hold values from -0.15625 to 0.15625
Outputs:
- hidden: bfloat16 [2, 4, 512, 1536], P('section', 'groups', 'seq', 'tp'), parts along dimension 1
There are 2 independent parts, one for each index of `groups`. A program takes and returns all parts, laid end to end along the dimension named above; an argument that names none is the same for every part. Nothing has to cross between parts.
Inputs may be any that keep to these rules, and one draw needn't show every extreme that they name: Each row of set_views sums to 8; every row has a set of 2 views.
All inputs are finite; a program needn't handle non-finite values.
Results may differ from a plain program's by a relative error of at most 0.01.
Values may be sent and summed in bfloat16 or wider, within the bound.
No kernel may reach another device: no remote copies, remote signals or barrier semaphores. Data moves between devices by JAX's collectives and lax.ppermute only.
A program may use at most 64 MiB of HBM per device.

v0:
```python
import jax
import jax.numpy as jnp
from jax import lax
from jax.sharding import PartitionSpec as P

REACH = 1
epsilon = 1e-06


def shifted(array, axis, by):
    size = lax.axis_size(axis)
    pairs = [(i, i + by) for i in range(size) if 0 <= i + by < size]
    return lax.ppermute(array, axis, pairs)


def view_sets(set_views, count):
    starts = jnp.cumsum(set_views) - set_views
    position = jnp.arange(count, dtype=jnp.int32)
    inside = (starts[None, :] <= position[:, None]).astype(jnp.int32)
    return jnp.sum(inside, axis=1) - 1


def unit_rms(values, scaling):
    return values * lax.rsqrt(jnp.mean(values * values, axis=-1, keepdims=True) + epsilon) * scaling


def relay_cycle(payload):
    moving = payload
    moving = shifted(moving, "seq", 1)
    below_list = [moving]
    moving = payload
    moving = shifted(moving, "seq", -1)
    above_list = [moving]
    return below_list[::-1] + [payload] + above_list


def body(stream, set_views, modulation, set_gate, qkv_weight, norm_gain, out_weight):
    micro_count, view_tok, local_width = stream.shape
    head_size = norm_gain.shape[2]
    head_count = local_width // head_size
    seq_count = lax.axis_size("seq")
    section_count = lax.axis_size("section")
    seq_place = lax.axis_index("seq")
    section_place = lax.axis_index("section")
    full_width = local_width * lax.axis_size("tp")
    whole_qkv = lax.all_gather(qkv_weight[0], "seq", axis=0, tiled=True)
    qkv_flat = whole_qkv.reshape(whole_qkv.shape[0], 3 * local_width)
    gain_pair = norm_gain[0]
    out_rows = out_weight[0]
    score_scale = head_size ** (-0.5)
    offsets = list(range(-REACH, REACH + 1))
    ticks = micro_count + section_count - 1
    carried = jnp.zeros((view_tok, local_width), jnp.bfloat16)
    hidden = jnp.zeros((micro_count, view_tok, local_width), jnp.bfloat16)
    for moment in range(ticks):
        fresh_input = stream[min(moment, micro_count - 1)]
        section_input = jnp.where(section_place == 0, fresh_input, carried)
        micro_raw = moment - section_place
        micro_index = jnp.clip(micro_raw, 0, micro_count - 1)
        owners = view_sets(set_views[micro_index], seq_count)
        own_set = owners[seq_place]
        widened = section_input.astype(jnp.float32)
        totals, squares = lax.psum(
            (jnp.sum(widened, axis=1), jnp.sum(widened * widened, axis=1)), "tp"
        )
        average = (totals / full_width)[:, None]
        spread = (squares / full_width)[:, None] - average * average
        factors = modulation[0, micro_index, own_set].astype(jnp.float32)
        normed = (
            (widened - average) * lax.rsqrt(spread + epsilon) * (1.0 + factors[1]) + factors[0]
        ).astype(jnp.bfloat16)
        section_projected = jnp.dot(
            lax.all_gather(normed, "tp", axis=1, tiled=True),
            qkv_flat,
            preferred_element_type=jnp.float32,
        )
        queries = unit_rms(
            section_projected.reshape(view_tok, 3, head_count, head_size)[:, 0], gain_pair[0]
        ).astype(jnp.bfloat16)
        parts = section_projected.reshape(view_tok, 3, head_count, head_size)
        keys_here = unit_rms(parts[:, 1], gain_pair[1]).astype(jnp.bfloat16)
        values_here = parts[:, 2].astype(jnp.bfloat16)
        key_list = []
        value_list = []
        stacked = jnp.stack(
            [keys_here.reshape(view_tok, local_width), values_here.reshape(view_tok, local_width)]
        )
        arrived = relay_cycle(stacked)
        for received in arrived:
            key_list.append(received[0].reshape(view_tok, head_count, head_size))
            value_list.append(received[1].reshape(view_tok, head_count, head_size))
        visible = []
        for offset in offsets:
            neighbour = seq_place + offset
            in_range = (neighbour >= 0) & (neighbour < seq_count)
            same_set = owners[jnp.clip(neighbour, 0, seq_count - 1)] == own_set
            visible.append((in_range & same_set).astype(jnp.float32))
        keys_cat = jnp.concatenate(key_list, axis=0)
        values_cat = jnp.concatenate(value_list, axis=0)
        mask_row = jnp.repeat(jnp.stack(visible), view_tok)
        scores = (
            jnp.einsum("qhd,khd->hqk", queries, keys_cat, preferred_element_type=jnp.float32)
            * score_scale
        )
        exponent = jnp.exp(scores) * mask_row
        denominator = jnp.sum(exponent, axis=-1)
        numerator = jnp.einsum(
            "hqk,khd->qhd",
            exponent.astype(jnp.bfloat16),
            values_cat,
            preferred_element_type=jnp.float32,
        )
        attended = (
            (numerator / jnp.transpose(denominator)[:, :, None])
            .astype(jnp.bfloat16)
            .reshape(view_tok, local_width)
        )
        mixed_out = jnp.dot(
            lax.all_gather(attended, "tp", axis=1, tiled=True),
            out_rows,
            preferred_element_type=jnp.float32,
        )
        gating = set_gate[0, micro_index, own_set].astype(jnp.float32)
        result = (widened + gating * mixed_out).astype(jnp.bfloat16)
        in_range = (micro_raw >= 0) & (micro_raw < micro_count)
        hidden = jnp.where(in_range, hidden.at[micro_index].set(result), hidden)
        if moment + 1 < ticks:
            carried = shifted(result, "section", 1)
    return hidden[None]


def solution(mesh):
    placed = (
        P("groups", "seq", "tp"),
        P("groups", None),
        P("section", "groups", None, None, "tp"),
        P("section", "groups", None, "tp"),
        P("section", "seq", None, "tp"),
        P("section", None, None),
        P("section", None, "tp"),
    )
    return jax.shard_map(
        body,
        mesh=mesh,
        in_specs=placed,
        out_specs=P("section", "groups", "seq", "tp"),
        check_vma=False,
    )
```

profile of v0, /device:TPU:10, one launch (start us, length us, event | category | flops | bytes accessed | tf_op | source)
XLA Modules:
  0.0 268.0 jit_solution(7791036206823551094)
XLA Ops:
  25.9 111.1 %all-gather.3.cloned.1.call-done = bf16[1,1536,3,1536]{3,1,2,0:T(8,128)(2,1)} async-done(((bf16[1,192,3,1536]{3,1,2,0:T(8,128)(2,1)}), bf16[1,1536,3,1536]{3,1,2,0:T(8,128)(2,1)}) %all-gather.3.cloned.1.call-update) | async-done | bytes 14155792 | tf_op jit(solution)/shard_map/all_gather | solution.py:46
  137.0 18.7 %copy.58 = bf16[1,1536,3,1536]{1,3,2,0:T(8,128)(2,1)} copy(bf16[1,1536,3,1536]{3,1,2,0:T(8,128)(2,1)} %all-gather.3.cloned.1.call-done) | data formatting | bytes 28311552 | tf_op jit(solution)/shard_map/all_gather | solution.py:46
  155.7 7.6 %fusion.129 = f32[64,3,12,128]{3,0,2,1:T(8,128)S(1)} fusion(bf16[3,12,128,1536]{3,2,1,0:T(8,128)(2,1)} %bitcast.253, f32[1536]{0:T(1024)S(1)} %get-tuple-element.59, f32[1536]{0:T(1024)S(1)} %get-tuple-element.58, f32[64]{0:T(128)S(1)} %get-tuple-element.102, f32[64]{0:T(128)S(1)} %get-tuple-element.101, bf16[2,64,1536]{2,1,0:T(8,128)(2,1)S(1)} %copy-done.6, ...), kind=kOutput, calls=%fused_computation.139 | convolution fusion | flops 906657792 | bytes 15549441 | tf_op jit(solution)/shard_map/dot_general | solution.py:72
  166.1 5.2 %collective-permute-start.1 = (bf16[2,64,1536]{2,1,0:T(8,128)(2,1)S(1)}, bf16[2,64,1536]{2,1,0:T(8,128)(2,1)S(1)}, u32[]{:S(2)}, u32[]{:S(2)}) collective-permute-start(bf16[2,64,1536]{2,1,0:T(8,128)(2,1)S(1)} %pad_maximum_fusion), channel_id=1, source_target_pairs={{2,0},{4,2},{6,4},{8,6},{10,8},{12,10},{14,12},{3,1},{5,3},{7,5},{... | collective-permute-start | bytes 1179656 | tf_op jit(solution)/shard_map/ppermute | solution.py:13
  171.3 1.9 collective-permute-start
  173.2 0.8 fusion.117
  174.1 2.5 collective-permute-done.1
  177.0 3.4 %collective-permute-done = bf16[2,64,1536]{2,1,0:T(8,128)(2,1)S(1)} collective-permute-done((bf16[2,64,1536]{2,1,0:T(8,128)(2,1)S(1)}, bf16[2,64,1536]{2,1,0:T(8,128)(2,1)S(1)}, u32[]{:S(2)}, u32[]{:S(2)}) %collective-permute-start) | collective-permute-done | bytes 393248 | tf_op jit(solution)/shard_map/ppermute | solution.py:13
  182.6 3.9 %bitcast_dynamic-update-slice_fusion = (bf16[2,64,1536]{2,1,0:T(8,128)(2,1)S(1)}, bf16[64,1536]{1,0:T(8,128)(2,1)S(1)}) fusion(bf16[2,64,1536]{2,1,0:T(8,128)(2,1)S(1)} %broadcast_in_dim.16, s32[]{:T(128)} %min.31, pred[]{:T(512)} %get-tuple-element.90, pred[]{:T(512)S(6)} %and.71, bf16[1,1536,1536]{2,1,0:T(8,128)(2,1)} %param.19, ...), kind=kOutput, calls=%fused_computation.148 | convolution fusion | flops 302678016 | bytes 5513223 | tf_op jit(solution)/shard_map/dot_general | solution.py:118
  186.5 1.3 collective-permute-start.2
  191.6 2.5 collective-permute-done.2
  194.3 7.6 %fusion.126 = f32[64,3,12,128]{3,0,2,1:T(8,128)S(1)} fusion(bf16[3,12,128,1536]{3,2,1,0:T(8,128)(2,1)} %bitcast.254, bf16[64,1536]{1,0:T(8,128)(2,1)S(1)} %get-tuple-element.63, f32[1536]{0:T(1024)S(1)} %get-tuple-element.57, f32[1536]{0:T(1024)S(1)} %get-tuple-element.56, f32[64]{0:T(128)S(1)} %get-tuple-element.96, f32[64]{0:T(128)S(1)} %get-tuple-element.95), kind=kOutput, calls=%fused_computation.137 | convolution fusion | flops 906559488 | bytes 15544832 | tf_op jit(solution)/shard_map/dot_general | solution.py:72
  203.2 0.8 convert_element_type.230
  204.7 1.0 pad_maximum_fusion.1
  205.7 1.9 collective-permute-start.4
  207.7 2.4 collective-permute-start.3
  210.1 0.8 fusion.114
  211.0 2.0 collective-permute-done.4
  214.1 2.8 %collective-permute-done.3 = bf16[2,64,1536]{2,1,0:T(8,128)(2,1)} collective-permute-done((bf16[2,64,1536]{2,1,0:T(8,128)(2,1)S(1)}, bf16[2,64,1536]{2,1,0:T(8,128)(2,1)}, u32[]{:S(2)}, u32[]{:S(2)}) %collective-permute-start.3) | collective-permute-done | bytes 393248 | tf_op jit(solution)/shard_map/ppermute | solution.py:13
  216.9 1.0 fusion.167
  218.4 1.6 fusion.175
  220.3 4.0 %fusion.121 = (bf16[2,64,1536]{2,1,0:T(8,128)(2,1)S(1)}, bf16[64,1536]{1,0:T(8,128)(2,1)S(1)}) fusion(bf16[2,64,1536]{2,1,0:T(8,128)(2,1)S(1)} %get-tuple-element.107, s32[]{:T(128)} %min.36, pred[]{:T(512)} %get-tuple-element.61, pred[]{:T(512)S(6)} %and.79, bf16[1,1536,1536]{2,1,0:T(8,128)(2,1)} %param.19, bf16[12,8,8,128]{3,2,1,0:T(8,128)(2,1)S(1)} %fusion.61, ...), kind=kOutput, calls=%fused_computation.133 | convolution fusion | flops 302579712 | bytes 5709830 | tf_op jit(solution)/shard_map/dot_general | solution.py:118
  224.3 1.5 collective-permute-start.5
  226.8 5.1 %collective-permute-done.5 = bf16[64,1536]{1,0:T(8,128)(2,1)S(1)} collective-permute-done((bf16[64,1536]{1,0:T(8,128)(2,1)S(1)}, bf16[64,1536]{1,0:T(8,128)(2,1)S(1)}, u32[]{:S(2)}, u32[]{:S(2)}) %collective-permute-start.5) | collective-permute-done | bytes 196640 | tf_op jit(solution)/shard_map/ppermute | solution.py:13
  232.1 7.6 %fusion.123 = f32[64,3,12,128]{3,0,2,1:T(8,128)S(1)} fusion(bf16[3,12,128,1536]{3,2,1,0:T(8,128)(2,1)} %bitcast.255, bf16[64,1536]{1,0:T(8,128)(2,1)S(1)} %get-tuple-element.62, f32[1536]{0:T(1024)S(1)} %get-tuple-element.55, f32[1536]{0:T(1024)S(1)} %get-tuple-element.54, f32[64]{0:T(128)S(1)} %get-tuple-element.89, f32[64]{0:T(128)S(1)} %get-tuple-element.88), kind=kOutput, calls=%fused_computation.135 | convolution fusion | flops 906559488 | bytes 15544832 | tf_op jit(solution)/shard_map/dot_general | solution.py:72
  242.5 2.1 collective-permute-start.7
  244.5 2.4 collective-permute-start.6
  247.0 0.8 fusion.111
  247.8 2.0 collective-permute-done.7
  251.6 2.0 collective-permute-done.6
  254.6 1.6 fusion.176
  256.5 4.6 %fusion.45 = bf16[1,2,64,1536]{3,2,1,0:T(8,128)(2,1)} fusion(bf16[1,2,64,1536]{3,2,1,0:T(8,128)(2,1)} %copy.110, s32[]{:T(128)} %min.38, bf16[1,1536,1536]{2,1,0:T(8,128)(2,1)} %param.19, bf16[64,1536]{1,0:T(8,128)(2,1)S(1)} %get-tuple-element.62, bf16[12,8,8,128]{3,2,1,0:T(8,128)(2,1)S(1)} %fusion.62, bf16[2,64,1536]{2,1,0:T(8,128)(2,1)S(1)} %get-tuple-element.109, ...), kind=kOutput, calls=%fused_computation.19 | convolution fusion | flops 302579712 | bytes 5512193 | tf_op jit(solution)/shard_map/dot_general | solution.py:118
  (158 shorter events, 22.4 us)
Async XLA Ops:
  6.5 17.4 %copy-start.17 = (s32[3]{0:T(128)S(1)}, s32[3]{0:T(128)}, u32[]{:S(2)}) copy-start(s32[3]{0:T(128)} %constant.115.clone.1) | copy-start | bytes 40
  6.5 0.8 copy-start.15
  6.5 17.3 %copy-start.14 = (bf16[1,2,6,1536]{3,1,2,0:T(2,128)(2,1)S(1)}, bf16[1,2,6,1536]{3,1,2,0:T(2,128)(2,1)}, u32[]{:S(2)}) copy-start(bf16[1,2,6,1536]{3,1,2,0:T(2,128)(2,1)} %param.16) | copy-start | bytes 110596
  6.5 19.0 %copy-start.6 = (bf16[2,64,1536]{2,1,0:T(8,128)(2,1)S(1)}, bf16[2,64,1536]{2,1,0:T(8,128)(2,1)}, u32[]{:S(2)}) copy-start(bf16[2,64,1536]{2,1,0:T(8,128)(2,1)} %param.13) | copy-start | bytes 1179652
  6.5 19.4 %copy-start.16 = (f32[1,2,128]{2,1,0:T(2,128)S(1)}, f32[1,2,128]{2,1,0:T(2,128)}, u32[]{:S(2)}) copy-start(f32[1,2,128]{2,1,0:T(2,128)} %param.18) | copy-start | bytes 3076
  6.5 130.5 %all-gather.3.cloned.1.call-start = ((), (), s32[]{:S(2)}) async-start(), calls=%async_computation | async-start | bytes 15925248 | tf_op jit(solution)/shard_map/all_gather | solution.py:46
  163.3 1.1 copy-start.2
  164.4 1.0 slice-start.1
  165.9 7.3 %copy-start.3 = (f32[64,3,12,128]{3,0,2,1:T(8,128)S(1)}, f32[64,3,12,128]{3,0,2,1:T(8,128)}, u32[]{:S(2)}) copy-start(f32[64,3,12,128]{3,0,2,1:T(8,128)} %copy-done.2) | copy-start | bytes 3538948
  166.1 10.5 %collective-permute-start.1 = (bf16[2,64,1536]{2,1,0:T(8,128)(2,1)S(1)}, bf16[2,64,1536]{2,1,0:T(8,128)(2,1)S(1)}, u32[]{:S(2)}, u32[]{:S(2)}) collective-permute-start(bf16[2,64,1536]{2,1,0:T(8,128)(2,1)S(1)} %pad_maximum_fusion), channel_id=1, source_target_pairs={{2,0},{4,2},{6,4},{8,6},{10,8},{12,10},{14,12},{3,1},{5,3},{7,5},{... | collective-permute-start | bytes 1179656 | tf_op jit(solution)/shard_map/ppermute | solution.py:13
  171.3 9.1 %collective-permute-start = (bf16[2,64,1536]{2,1,0:T(8,128)(2,1)S(1)}, bf16[2,64,1536]{2,1,0:T(8,128)(2,1)S(1)}, u32[]{:S(2)}, u32[]{:S(2)}) collective-permute-start(bf16[2,64,1536]{2,1,0:T(8,128)(2,1)S(1)} %pad_maximum_fusion), channel_id=1, source_target_pairs={{0,2},{2,4},{4,6},{6,8},{8,10},{10,12},{12,14},{1,3},{3,5},{5,7},{... | collective-permute-start | bytes 1179656 | tf_op jit(solution)/shard_map/ppermute | solution.py:13
  180.4 0.9 copy-start.13
  181.3 0.9 copy-start.11
  186.5 7.6 %collective-permute-start.2 = (bf16[64,1536]{1,0:T(8,128)(2,1)S(1)}, bf16[64,1536]{1,0:T(8,128)(2,1)S(1)}, u32[]{:S(2)}, u32[]{:S(2)}) collective-permute-start(bf16[64,1536]{1,0:T(8,128)(2,1)S(1)} %get-tuple-element.108), channel_id=1, source_target_pairs={{0,1},{2,3},{4,5},{6,7},{8,9},{10,11},{12,13},{14,15},{16,17},{18,... | collective-permute-start | bytes 589832 | tf_op jit(solution)/shard_map/ppermute | solution.py:13
  201.9 1.1 copy-start.4
  203.0 1.1 slice-start.2
  204.6 5.5 %copy-start.5 = (f32[64,3,12,128]{3,0,2,1:T(8,128)S(1)}, f32[64,3,12,128]{3,0,2,1:T(8,128)}, u32[]{:S(2)}) copy-start(f32[64,3,12,128]{3,0,2,1:T(8,128)} %copy-done.4) | copy-start | bytes 3538948
  205.7 7.2 %collective-permute-start.4 = (bf16[2,64,1536]{2,1,0:T(8,128)(2,1)S(1)}, bf16[2,64,1536]{2,1,0:T(8,128)(2,1)S(1)}, u32[]{:S(2)}, u32[]{:S(2)}) collective-permute-start(bf16[2,64,1536]{2,1,0:T(8,128)(2,1)S(1)} %pad_maximum_fusion.1), channel_id=1, source_target_pairs={{2,0},{4,2},{6,4},{8,6},{10,8},{12,10},{14,12},{3,1},{5,3},{7,5},{... | collective-permute-start | bytes 1179656 | tf_op jit(solution)/shard_map/ppermute | solution.py:13
  207.7 9.2 %collective-permute-start.3 = (bf16[2,64,1536]{2,1,0:T(8,128)(2,1)S(1)}, bf16[2,64,1536]{2,1,0:T(8,128)(2,1)}, u32[]{:S(2)}, u32[]{:S(2)}) collective-permute-start(bf16[2,64,1536]{2,1,0:T(8,128)(2,1)S(1)} %pad_maximum_fusion.1), channel_id=1, source_target_pairs={{0,2},{2,4},{4,6},{6,8},{8,10},{10,12},{12,14},{1,3},{3,5},{5,7},{... | collective-permute-start | bytes 1179656 | tf_op jit(solution)/shard_map/ppermute | solution.py:13
  218.4 1.6 copy-start.9
  218.4 1.6 copy-start.12
  224.3 7.6 %collective-permute-start.5 = (bf16[64,1536]{1,0:T(8,128)(2,1)S(1)}, bf16[64,1536]{1,0:T(8,128)(2,1)S(1)}, u32[]{:S(2)}, u32[]{:S(2)}) collective-permute-start(bf16[64,1536]{1,0:T(8,128)(2,1)S(1)} %get-tuple-element.110), channel_id=1, source_target_pairs={{0,1},{2,3},{4,5},{6,7},{8,9},{10,11},{12,13},{14,15},{16,17},{18,... | collective-permute-start | bytes 589832 | tf_op jit(solution)/shard_map/ppermute | solution.py:13
  239.7 1.1 copy-start
  240.8 1.0 slice-start
  242.3 4.7 %copy-start.1 = (f32[64,3,12,128]{3,0,2,1:T(8,128)S(1)}, f32[64,3,12,128]{3,0,2,1:T(8,128)}, u32[]{:S(2)}) copy-start(f32[64,3,12,128]{3,0,2,1:T(8,128)} %copy-done) | copy-start | bytes 3538948
  242.5 7.3 %collective-permute-start.7 = (bf16[2,64,1536]{2,1,0:T(8,128)(2,1)S(1)}, bf16[2,64,1536]{2,1,0:T(8,128)(2,1)S(1)}, u32[]{:S(2)}, u32[]{:S(2)}) collective-permute-start(bf16[2,64,1536]{2,1,0:T(8,128)(2,1)S(1)} %pad_maximum_fusion.2), channel_id=1, source_target_pairs={{2,0},{4,2},{6,4},{8,6},{10,8},{12,10},{14,12},{3,1},{5,3},{7,5},{... | collective-permute-start | bytes 1179656 | tf_op jit(solution)/shard_map/ppermute | solution.py:13
  244.5 9.1 %collective-permute-start.6 = (bf16[2,64,1536]{2,1,0:T(8,128)(2,1)S(1)}, bf16[2,64,1536]{2,1,0:T(8,128)(2,1)S(1)}, u32[]{:S(2)}, u32[]{:S(2)}) collective-permute-start(bf16[2,64,1536]{2,1,0:T(8,128)(2,1)S(1)} %pad_maximum_fusion.2), channel_id=1, source_target_pairs={{0,2},{2,4},{4,6},{6,8},{8,10},{10,12},{12,14},{1,3},{3,5},{5,7},{... | collective-permute-start | bytes 1179656 | tf_op jit(solution)/shard_map/ppermute | solution.py:13
  253.6 0.9 copy-start.7
  254.6 1.6 copy-start.8
  254.6 1.6 copy-start.10
Sparse Core Ops, SparseCore 0:
  9.0 128.0 all-gather.2
where the time goes:
time: 269 us; the launch traced here: 268 us
  waiting for transfers between devices  134 us (50%)
  matrix products  40 us (15%)
  local copies, waits for them, and re-layouts  35.9 us (13%)
  between operations  31.1 us (12%)
  starting transfers between devices  18.7 us (7%)
  other arithmetic  8.29 us (3%)
    all_gather x1, waiting for transfers between devices, body(): whole_qkv = lax.all_gather(qkv_weight[0], 'seq', axis=0, tiled=True)  111 us
    dot_general x3, matrix products, body(): jnp.dot(lax.all_gather(normed, 'tp', axis=1, tiled=True), qkv_flat, prefe...  22.7 us
    ppermute x8, waiting for transfers between devices, shifted(): return lax.ppermute(array, axis, pairs)  22.2 us
    all_gather x1, local copies, waits for them, and re-layouts, body(): whole_qkv = lax.all_gather(qkv_weight[0], 'seq', axis=0, tiled=True)  18.7 us
    ppermute x8, starting transfers between devices, shifted(): return lax.ppermute(array, axis, pairs)  18.7 us
    dot_general x3, matrix products, body(): jnp.dot(lax.all_gather(attended, 'tp', axis=1, tiled=True), out_rows, pre...  12.5 us
  transfers between devices with their start and end apart: 9, of which 9 were waited for; matrix products, arithmetic and copies ran while one was open for 5% of the time, Pallas kernels for 0%

commit v1 on v0

--- a/solution.py
+++ b/solution.py
@@ -43,7 +43,22 @@
     seq_place = lax.axis_index("seq")
     section_place = lax.axis_index("section")
     full_width = local_width * lax.axis_size("tp")
-    whole_qkv = lax.all_gather(qkv_weight[0], "seq", axis=0, tiled=True)
+    ways, here, step = (lax.axis_size("seq"), lax.axis_index("seq"), qkv_weight[0].shape[0])
+    lengths = [n * ways if d == 0 else n for d, n in enumerate(qkv_weight[0].shape)]
+    whole_qkv = lax.dynamic_update_slice_in_dim(
+        jnp.zeros(lengths, qkv_weight[0].dtype), qkv_weight[0], here * step, axis=0
+    )
+    going_up = going_down = qkv_weight[0]
+    for far in range(1, ways // 2 + 1):
+        going_up = lax.ppermute(going_up, "seq", [(d, (d + 1) % ways) for d in range(ways)])
+        whole_qkv = lax.dynamic_update_slice_in_dim(
+            whole_qkv, going_up, (here - far) % ways * step, axis=0
+        )
+        if 2 * far < ways:
+            going_down = lax.ppermute(going_down, "seq", [(d, (d - 1) % ways) for d in range(ways)])
+            whole_qkv = lax.dynamic_update_slice_in_dim(
+                whole_qkv, going_down, (here + far) % ways * step, axis=0
+            )
     qkv_flat = whole_qkv.reshape(whole_qkv.shape[0], 3 * local_width)
     gain_pair = norm_gain[0]
     out_rows = out_weight[0]

time: 269 us -> 458 us (1.70)
  the two profiles are of different devices: /device:TPU:10 before, /device:TPU:15 now
where the time goes in v1:
time: 458 us; the launch traced here: 452 us
  local copies, waits for them, and re-layouts  226 us (49%)
  waiting for transfers between devices  129 us (28%)
  matrix products  39 us (9%)
  starting transfers between devices  30.1 us (7%)
  between operations  18.2 us (4%)
  other arithmetic  9.63 us (2%)
    ppermute x4, waiting for transfers between devices, body(): lax.ppermute(going_up, 'seq', [(d, (d + 1) % ways) for d in range(ways)])  107 us
    dynamic_update_slice x4, local copies, waits for them, and re-layouts, body(): lax.dynamic_update_slice_in_dim(whole_qkv, going_up, (here - far) % ways...  91.3 us
    dynamic_update_slice x3, local copies, waits for them, and re-layouts, body(): lax.dynamic_update_slice_in_dim(whole_qkv, going_down, (here + far) % way...  67.3 us
    dynamic_update_slice x1, local copies, waits for them, and re-layouts, body(): lax.dynamic_update_slice_in_dim(jnp.zeros(lengths, qkv_weight[0].dtype),...  24.4 us
    dot_general x3, matrix products, body(): jnp.dot(lax.all_gather(normed, 'tp', axis=1, tiled=True), qkv_flat, prefe...  22.7 us
    ppermute x8, waiting for transfers between devices, shifted(): return lax.ppermute(array, axis, pairs)  22.5 us
    ppermute x8, starting transfers between devices, shifted(): return lax.ppermute(array, axis, pairs)  18 us
    dot_general x3, matrix products, body(): jnp.dot(lax.all_gather(attended, 'tp', axis=1, tiled=True), out_rows, pre...  12.5 us
  transfers between devices with their start and end apart: 15, of which 11 were waited for; matrix products, arithmetic and copies ran while one was open for 44% of the time, Pallas kernels for 0%

profile of v1, /device:TPU:15, one launch (start us, length us, event | category | flops | bytes accessed | tf_op | source)
XLA Modules:
  0.0 452.2 jit_solution(1176704365144102347)
XLA Ops:
  1.9 36.1 %collective-permute-done = bf16[192,3,1536]{2,0,1:T(8,128)(2,1)S(1)} collective-permute-done((bf16[192,3,1536]{2,0,1:T(8,128)(2,1)}, bf16[192,3,1536]{2,0,1:T(8,128)(2,1)S(1)}, u32[]{:S(2)}, u32[]{:S(2)}) %collective-permute-start) | collective-permute-done | bytes 1769504 | tf_op jit(solution)/shard_map/ppermute | solution.py:53
  38.0 5.0 %collective-permute-start.2 = (bf16[192,3,1536]{2,0,1:T(8,128)(2,1)S(1)}, bf16[192,3,1536]{2,0,1:T(8,128)(2,1)S(1)}, u32[]{:S(2)}, u32[]{:S(2)}) collective-permute-start(bf16[192,3,1536]{2,0,1:T(8,128)(2,1)S(1)} %collective-permute-done), channel_id=1, source_target_pairs={{0,2},{2,4},{4,6},{6,8},{8,10},{10,12},{12,14},{14,0},{1,3},{3,5},... | collective-permute-start | bytes 5308424 | tf_op jit(solution)/shard_map/ppermute | solution.py:53
  43.0 38.4 %collective-permute-done.2 = bf16[192,3,1536]{2,0,1:T(8,128)(2,1)S(1)} collective-permute-done((bf16[192,3,1536]{2,0,1:T(8,128)(2,1)S(1)}, bf16[192,3,1536]{2,0,1:T(8,128)(2,1)S(1)}, u32[]{:S(2)}, u32[]{:S(2)}) %collective-permute-start.2) | collective-permute-done | bytes 1769504 | tf_op jit(solution)/shard_map/ppermute | solution.py:53
  87.9 32.0 %collective-permute-done.4 = bf16[192,3,1536]{2,0,1:T(8,128)(2,1)} collective-permute-done((bf16[192,3,1536]{2,0,1:T(8,128)(2,1)S(1)}, bf16[192,3,1536]{2,0,1:T(8,128)(2,1)}, u32[]{:S(2)}, u32[]{:S(2)}) %collective-permute-start.4) | collective-permute-done | bytes 1769504 | tf_op jit(solution)/shard_map/ppermute | solution.py:53
  119.9 2.7 collective-permute-start.6
  122.8 2.7 copy.67
  141.2 6.2 %broadcast_in_dim.20 = bf16[1536,3,1536]{0,2,1:T(8,128)(2,1)} broadcast(bf16[]{:T(256)} %constant.151.clone.1), dimensions={} | broadcast | bytes 14155778 | tf_op jit(solution)/shard_map/broadcast_in_dim | solution.py:49
  147.4 24.4 %dynamic_update_slice.24 = bf16[1536,3,1536]{0,2,1:T(8,128)(2,1)} dynamic-update-slice(bf16[1536,3,1536]{0,2,1:T(8,128)(2,1)} %broadcast_in_dim.20, bf16[192,3,1536]{0,2,1:T(8,128)(2,1)S(1)} %bitcast.259, s32[]{:T(128)S(6)} %select_n.146, s32[]{:T(128)} %constant.152.clone.1, s32[]{:T(128)} %constant.152.clone.1) | dynamic-update-slice | bytes 3538948 | tf_op jit(solution)/shard_map/dynamic_update_slice | solution.py:48
  173.9 2.7 copy.69
  176.6 21.8 %dynamic_update_slice.25 = bf16[1536,3,1536]{0,2,1:T(8,128)(2,1)} dynamic-update-slice(bf16[1536,3,1536]{0,2,1:T(8,128)(2,1)} %dynamic_update_slice.24, bf16[192,3,1536]{0,2,1:T(8,128)(2,1)S(1)} %copy.69, s32[]{:T(128)S(6)} %select_n.148, s32[]{:T(128)} %constant.152.clone.1, s32[]{:T(128)} %constant.152.clone.1) | dynamic-update-slice | bytes 3538948 | tf_op jit(solution)/shard_map/dynamic_update_slice | solution.py:54
  198.4 2.7 copy.71
  201.0 21.9 %dynamic_update_slice.26 = bf16[1536,3,1536]{0,2,1:T(8,128)(2,1)} dynamic-update-slice(bf16[1536,3,1536]{0,2,1:T(8,128)(2,1)} %dynamic_update_slice.25, bf16[192,3,1536]{0,2,1:T(8,128)(2,1)S(1)} %copy.71, s32[]{:T(128)S(6)} %select_n.150, s32[]{:T(128)} %constant.152.clone.1, s32[]{:T(128)} %constant.152.clone.1) | dynamic-update-slice | bytes 3538948 | tf_op jit(solution)/shard_map/dynamic_update_slice | solution.py:59
  222.9 2.7 copy.72
  225.6 24.4 %dynamic_update_slice.27 = bf16[1536,3,1536]{0,2,1:T(8,128)(2,1)} dynamic-update-slice(bf16[1536,3,1536]{0,2,1:T(8,128)(2,1)} %dynamic_update_slice.26, bf16[192,3,1536]{0,2,1:T(8,128)(2,1)S(1)} %copy.72, s32[]{:T(128)S(6)} %select_n.152, s32[]{:T(128)} %constant.152.clone.1, s32[]{:T(128)} %constant.152.clone.1) | dynamic-update-slice | bytes 3538948 | tf_op jit(solution)/shard_map/dynamic_update_slice | solution.py:54
  252.7 24.4 %dynamic_update_slice.28 = bf16[1536,3,1536]{0,2,1:T(8,128)(2,1)} dynamic-update-slice(bf16[1536,3,1536]{0,2,1:T(8,128)(2,1)} %dynamic_update_slice.27, bf16[192,3,1536]{0,2,1:T(8,128)(2,1)S(1)} %copy.73, s32[]{:T(128)S(6)} %select_n.154, s32[]{:T(128)} %constant.152.clone.1, s32[]{:T(128)} %constant.152.clone.1) | dynamic-update-slice | bytes 3538948 | tf_op jit(solution)/shard_map/dynamic_update_slice | solution.py:59
  279.7 21.7 %dynamic_update_slice.29 = bf16[1536,3,1536]{0,2,1:T(8,128)(2,1)} dynamic-update-slice(bf16[1536,3,1536]{0,2,1:T(8,128)(2,1)} %dynamic_update_slice.28, bf16[192,3,1536]{0,2,1:T(8,128)(2,1)S(1)} %copy.74, s32[]{:T(128)S(6)} %select_n.156, s32[]{:T(128)} %constant.152.clone.1, s32[]{:T(128)} %constant.152.clone.1) | dynamic-update-slice | bytes 3538948 | tf_op jit(solution)/shard_map/dynamic_update_slice | solution.py:54
  301.4 2.7 copy.75
  304.1 21.1 %dynamic_update_slice.30 = bf16[1536,3,1536]{0,2,1:T(8,128)(2,1)} dynamic-update-slice(bf16[1536,3,1536]{0,2,1:T(8,128)(2,1)} %dynamic_update_slice.29, bf16[192,3,1536]{0,2,1:T(8,128)(2,1)S(1)} %copy.75, s32[]{:T(128)S(6)} %select_n.158, s32[]{:T(128)} %constant.152.clone.1, s32[]{:T(128)} %constant.152.clone.1) | dynamic-update-slice | bytes 3538948 | tf_op jit(solution)/shard_map/dynamic_update_slice | solution.py:59
  325.2 2.7 copy.76
  327.9 23.5 %dynamic_update_slice.31 = bf16[1536,3,1536]{0,2,1:T(8,128)(2,1)} dynamic-update-slice(bf16[1536,3,1536]{0,2,1:T(8,128)(2,1)} %dynamic_update_slice.30, bf16[192,3,1536]{0,2,1:T(8,128)(2,1)S(1)} %copy.76, s32[]{:T(128)S(6)} %select_n.160, s32[]{:T(128)} %constant.152.clone.1, s32[]{:T(128)} %constant.152.clone.1) | dynamic-update-slice | bytes 3538948 | tf_op jit(solution)/shard_map/dynamic_update_slice | solution.py:54
  351.4 7.5 %fusion.129 = f32[64,3,12,128]{3,0,2,1:T(8,128)S(1)} fusion(bf16[3,12,128,1536]{3,2,1,0:T(8,128)(2,1)} %bitcast.256, f32[1536]{0:T(1024)S(1)} %get-tuple-element.59, f32[1536]{0:T(1024)S(1)} %get-tuple-element.58, f32[64]{0:T(128)S(1)} %get-tuple-element.102, f32[64]{0:T(128)S(1)} %get-tuple-element.101, bf16[2,64,1536]{2,1,0:T(8,128)(2,1)S(1)} %copy-done, ...), kind=kOutput, calls=%fused_computation.139 | convolution fusion | flops 906657792 | bytes 15549441 | tf_op jit(solution)/shard_map/dot_general | solution.py:87
  367.2 4.2 collective-permute-done.8
  373.5 3.9 bitcast_dynamic-update-slice_fusion
  385.2 7.6 %fusion.126 = f32[64,3,12,128]{3,0,2,1:T(8,128)S(1)} fusion(bf16[3,12,128,1536]{3,2,1,0:T(8,128)(2,1)} %bitcast.257, bf16[64,1536]{1,0:T(8,128)(2,1)S(1)} %get-tuple-element.63, f32[1536]{0:T(1024)S(1)} %get-tuple-element.57, f32[1536]{0:T(1024)S(1)} %get-tuple-element.56, f32[64]{0:T(128)S(1)} %get-tuple-element.96, f32[64]{0:T(128)S(1)} %get-tuple-element.95), kind=kOutput, calls=%fused_computation.137 | convolution fusion | flops 906559488 | bytes 15544832 | tf_op jit(solution)/shard_map/dot_general | solution.py:87
  395.8 3.0 collective-permute-start.10
  403.7 4.3 collective-permute-done.11
  411.6 4.0 fusion.121
  417.9 5.0 %collective-permute-done.12 = bf16[64,1536]{1,0:T(8,128)(2,1)S(1)} collective-permute-done((bf16[64,1536]{1,0:T(8,128)(2,1)S(1)}, bf16[64,1536]{1,0:T(8,128)(2,1)S(1)}, u32[]{:S(2)}, u32[]{:S(2)}) %collective-permute-start.12) | collective-permute-done | bytes 196640 | tf_op jit(solution)/shard_map/ppermute | solution.py:13
  423.1 7.6 %fusion.123 = f32[64,3,12,128]{3,0,2,1:T(8,128)S(1)} fusion(bf16[3,12,128,1536]{3,2,1,0:T(8,128)(2,1)} %bitcast.258, bf16[64,1536]{1,0:T(8,128)(2,1)S(1)} %get-tuple-element.62, f32[1536]{0:T(1024)S(1)} %get-tuple-element.55, f32[1536]{0:T(1024)S(1)} %get-tuple-element.54, f32[64]{0:T(128)S(1)} %get-tuple-element.89, f32[64]{0:T(128)S(1)} %get-tuple-element.88), kind=kOutput, calls=%fused_computation.135 | convolution fusion | flops 906559488 | bytes 15544832 | tf_op jit(solution)/shard_map/dot_general | solution.py:87
  432.1 3.9 collective-permute-start.13
  441.7 3.5 collective-permute-done.14
  447.6 4.6 %fusion.45 = bf16[1,2,64,1536]{3,2,1,0:T(8,128)(2,1)} fusion(bf16[1,2,64,1536]{3,2,1,0:T(8,128)(2,1)} %copy.138, s32[]{:T(128)} %min.38, bf16[1,1536,1536]{2,1,0:T(8,128)(2,1)} %param.19, bf16[64,1536]{1,0:T(8,128)(2,1)S(1)} %get-tuple-element.62, bf16[12,8,8,128]{3,2,1,0:T(8,128)(2,1)S(1)} %fusion.62, bf16[2,64,1536]{2,1,0:T(8,128)(2,1)S(1)} %get-tuple-element.109, ...), kind=kOutput, calls=%fused_computation.19 | convolution fusion | flops 302579712 | bytes 5512193 | tf_op jit(solution)/shard_map/dot_general | solution.py:133
  (170 shorter events, 55.5 us)
Async XLA Ops:
  0.0 38.0 %collective-permute-start = (bf16[192,3,1536]{2,0,1:T(8,128)(2,1)}, bf16[192,3,1536]{2,0,1:T(8,128)(2,1)S(1)}, u32[]{:S(2)}, u32[]{:S(2)}) collective-permute-start(bf16[192,3,1536]{2,0,1:T(8,128)(2,1)} %bitcast.261), channel_id=1, source_target_pairs={{0,2},{2,4},{4,6},{6,8},{8,10},{10,12},{12,14},{14,0},{1,3},{3,5},... | collective-permute-start | bytes 5308424 | tf_op jit(solution)/shard_map/ppermute | solution.py:53
  1.9 41.1 %collective-permute-start.1 = (bf16[192,3,1536]{2,0,1:T(8,128)(2,1)}, bf16[192,3,1536]{2,0,1:T(8,128)(2,1)S(1)}, u32[]{:S(2)}, u32[]{:S(2)}) collective-permute-start(bf16[192,3,1536]{2,0,1:T(8,128)(2,1)} %bitcast.262), channel_id=1, source_target_pairs={{0,14},{2,0},{4,2},{6,4},{8,6},{10,8},{12,10},{14,12},{1,15},{3,1}... | collective-permute-start | bytes 5308424 | tf_op jit(solution)/shard_map/ppermute | solution.py:58
  38.0 43.5 %copy-start.3 = (bf16[192,3,1536]{2,0,1:T(8,128)(2,1)}, bf16[192,3,1536]{2,0,1:T(8,128)(2,1)S(1)}, u32[]{:S(2)}) copy-start(bf16[192,3,1536]{2,0,1:T(8,128)(2,1)S(1)} %collective-permute-done) | copy-start | bytes 5308420
  38.0 43.4 %collective-permute-start.2 = (bf16[192,3,1536]{2,0,1:T(8,128)(2,1)S(1)}, bf16[192,3,1536]{2,0,1:T(8,128)(2,1)S(1)}, u32[]{:S(2)}, u32[]{:S(2)}) collective-permute-start(bf16[192,3,1536]{2,0,1:T(8,128)(2,1)S(1)} %collective-permute-done), channel_id=1, source_target_pairs={{0,2},{2,4},{4,6},{6,8},{8,10},{10,12},{12,14},{14,0},{1,3},{3,5},... | collective-permute-start | bytes 5308424 | tf_op jit(solution)/shard_map/ppermute | solution.py:53
  43.0 79.8 %copy-start.1 = (bf16[192,3,1536]{2,0,1:T(8,128)(2,1)}, bf16[192,3,1536]{2,0,1:T(8,128)(2,1)S(1)}, u32[]{:S(2)}) copy-start(bf16[192,3,1536]{2,0,1:T(8,128)(2,1)S(1)} %collective-permute-done.1) | copy-start | bytes 5308420
  43.0 44.9 %collective-permute-start.3 = (bf16[192,3,1536]{2,0,1:T(8,128)(2,1)S(1)}, bf16[192,3,1536]{2,0,1:T(8,128)(2,1)}, u32[]{:S(2)}, u32[]{:S(2)}) collective-permute-start(bf16[192,3,1536]{2,0,1:T(8,128)(2,1)S(1)} %collective-permute-done.1), channel_id=1, source_target_pairs={{0,14},{2,0},{4,2},{6,4},{8,6},{10,8},{12,10},{14,12},{1,15},{3,1}... | collective-permute-start | bytes 5308424 | tf_op jit(solution)/shard_map/ppermute | solution.py:58
  81.4 41.3 %copy-start.2 = (bf16[192,3,1536]{2,0,1:T(8,128)(2,1)}, bf16[192,3,1536]{2,0,1:T(8,128)(2,1)S(1)}, u32[]{:S(2)}) copy-start(bf16[192,3,1536]{2,0,1:T(8,128)(2,1)S(1)} %collective-permute-done.2) | copy-start | bytes 5308420
  81.4 38.5 %collective-permute-start.4 = (bf16[192,3,1536]{2,0,1:T(8,128)(2,1)S(1)}, bf16[192,3,1536]{2,0,1:T(8,128)(2,1)}, u32[]{:S(2)}, u32[]{:S(2)}) collective-permute-start(bf16[192,3,1536]{2,0,1:T(8,128)(2,1)S(1)} %collective-permute-done.2), channel_id=1, source_target_pairs={{0,2},{2,4},{4,6},{6,8},{8,10},{10,12},{12,14},{14,0},{1,3},{3,5},... | collective-permute-start | bytes 5308424 | tf_op jit(solution)/shard_map/ppermute | solution.py:53
  87.9 213.5 %collective-permute-start.5 = (bf16[192,3,1536]{2,0,1:T(8,128)(2,1)}, bf16[192,3,1536]{2,0,1:T(8,128)(2,1)}, u32[]{:S(2)}, u32[]{:S(2)}) collective-permute-start(bf16[192,3,1536]{2,0,1:T(8,128)(2,1)} %collective-permute-done.3), channel_id=1, source_target_pairs={{0,14},{2,0},{4,2},{6,4},{8,6},{10,8},{12,10},{14,12},{1,15},{3,1}... | collective-permute-start | bytes 5308424 | tf_op jit(solution)/shard_map/ppermute | solution.py:58
  119.9 205.3 %collective-permute-start.6 = (bf16[192,3,1536]{2,0,1:T(8,128)(2,1)}, bf16[192,3,1536]{2,0,1:T(8,128)(2,1)}, u32[]{:S(2)}, u32[]{:S(2)}) collective-permute-start(bf16[192,3,1536]{2,0,1:T(8,128)(2,1)} %collective-permute-done.4), channel_id=1, source_target_pairs={{0,2},{2,4},{4,6},{6,8},{8,10},{10,12},{12,14},{14,0},{1,3},{3,5},... | collective-permute-start | bytes 5308424 | tf_op jit(solution)/shard_map/ppermute | solution.py:53
  147.4 24.4 %copy-start.9 = (bf16[1,2,6,1536]{3,1,2,0:T(2,128)(2,1)S(1)}, bf16[1,2,6,1536]{3,1,2,0:T(2,128)(2,1)}, u32[]{:S(2)}) copy-start(bf16[1,2,6,1536]{3,1,2,0:T(2,128)(2,1)} %param.16) | copy-start | bytes 110596
  147.4 24.5 %copy-start.11 = (s32[3]{0:T(128)S(1)}, s32[3]{0:T(128)}, u32[]{:S(2)}) copy-start(s32[3]{0:T(128)} %constant.157.clone.1) | copy-start | bytes 40
  147.4 26.1 %copy-start = (bf16[2,64,1536]{2,1,0:T(8,128)(2,1)S(1)}, bf16[2,64,1536]{2,1,0:T(8,128)(2,1)}, u32[]{:S(2)}) copy-start(bf16[2,64,1536]{2,1,0:T(8,128)(2,1)} %param.13) | copy-start | bytes 1179652
  147.4 26.4 %copy-start.10 = (f32[1,2,128]{2,1,0:T(2,128)S(1)}, f32[1,2,128]{2,1,0:T(2,128)}, u32[]{:S(2)}) copy-start(f32[1,2,128]{2,1,0:T(2,128)} %param.18) | copy-start | bytes 3076
  360.3 6.6 %collective-permute-start.7 = (bf16[2,64,1536]{2,1,0:T(8,128)(2,1)S(1)}, bf16[2,64,1536]{2,1,0:T(8,128)(2,1)S(1)}, u32[]{:S(2)}, u32[]{:S(2)}) collective-permute-start(bf16[2,64,1536]{2,1,0:T(8,128)(2,1)S(1)} %pad_maximum_fusion), channel_id=1, source_target_pairs={{0,2},{2,4},{4,6},{6,8},{8,10},{10,12},{12,14},{1,3},{3,5},{5,7},{... | collective-permute-start | bytes 1179656 | tf_op jit(solution)/shard_map/ppermute | solution.py:13
  362.3 9.2 %collective-permute-start.8 = (bf16[2,64,1536]{2,1,0:T(8,128)(2,1)S(1)}, bf16[2,64,1536]{2,1,0:T(8,128)(2,1)S(1)}, u32[]{:S(2)}, u32[]{:S(2)}) collective-permute-start(bf16[2,64,1536]{2,1,0:T(8,128)(2,1)S(1)} %pad_maximum_fusion), channel_id=1, source_target_pairs={{2,0},{4,2},{6,4},{8,6},{10,8},{12,10},{14,12},{3,1},{5,3},{7,5},{... | collective-permute-start | bytes 1179656 | tf_op jit(solution)/shard_map/ppermute | solution.py:13
  371.6 0.9 copy-start.8
  377.4 7.5 %collective-permute-start.9 = (bf16[64,1536]{1,0:T(8,128)(2,1)S(1)}, bf16[64,1536]{1,0:T(8,128)(2,1)S(1)}, u32[]{:S(2)}, u32[]{:S(2)}) collective-permute-start(bf16[64,1536]{1,0:T(8,128)(2,1)S(1)} %get-tuple-element.108), channel_id=1, source_target_pairs={{0,1},{2,3},{4,5},{6,7},{8,9},{10,11},{12,13},{14,15},{16,17},{18,... | collective-permute-start | bytes 589832 | tf_op jit(solution)/shard_map/ppermute | solution.py:13
  395.8 7.7 %collective-permute-start.10 = (bf16[2,64,1536]{2,1,0:T(8,128)(2,1)S(1)}, bf16[2,64,1536]{2,1,0:T(8,128)(2,1)S(1)}, u32[]{:S(2)}, u32[]{:S(2)}) collective-permute-start(bf16[2,64,1536]{2,1,0:T(8,128)(2,1)S(1)} %pad_maximum_fusion.1), channel_id=1, source_target_pairs={{0,2},{2,4},{4,6},{6,8},{8,10},{10,12},{12,14},{1,3},{3,5},{5,7},{... | collective-permute-start | bytes 1179656 | tf_op jit(solution)/shard_map/ppermute | solution.py:13
  398.7 9.2 %collective-permute-start.11 = (bf16[2,64,1536]{2,1,0:T(8,128)(2,1)S(1)}, bf16[2,64,1536]{2,1,0:T(8,128)(2,1)}, u32[]{:S(2)}, u32[]{:S(2)}) collective-permute-start(bf16[2,64,1536]{2,1,0:T(8,128)(2,1)S(1)} %pad_maximum_fusion.1), channel_id=1, source_target_pairs={{2,0},{4,2},{6,4},{8,6},{10,8},{12,10},{14,12},{3,1},{5,3},{7,5},{... | collective-permute-start | bytes 1179656 | tf_op jit(solution)/shard_map/ppermute | solution.py:13
  409.6 1.6 copy-start.6
  415.6 7.4 %collective-permute-start.12 = (bf16[64,1536]{1,0:T(8,128)(2,1)S(1)}, bf16[64,1536]{1,0:T(8,128)(2,1)S(1)}, u32[]{:S(2)}, u32[]{:S(2)}) collective-permute-start(bf16[64,1536]{1,0:T(8,128)(2,1)S(1)} %get-tuple-element.110), channel_id=1, source_target_pairs={{0,1},{2,3},{4,5},{6,7},{8,9},{10,11},{12,13},{14,15},{16,17},{18,... | collective-permute-start | bytes 589832 | tf_op jit(solution)/shard_map/ppermute | solution.py:13
  432.1 8.6 %collective-permute-start.13 = (bf16[2,64,1536]{2,1,0:T(8,128)(2,1)S(1)}, bf16[2,64,1536]{2,1,0:T(8,128)(2,1)S(1)}, u32[]{:S(2)}, u32[]{:S(2)}) collective-permute-start(bf16[2,64,1536]{2,1,0:T(8,128)(2,1)S(1)} %pad_maximum_fusion.2), channel_id=1, source_target_pairs={{0,2},{2,4},{4,6},{6,8},{8,10},{10,12},{12,14},{1,3},{3,5},{5,7},{... | collective-permute-start | bytes 1179656 | tf_op jit(solution)/shard_map/ppermute | solution.py:13
  436.0 9.1 %collective-permute-start.14 = (bf16[2,64,1536]{2,1,0:T(8,128)(2,1)S(1)}, bf16[2,64,1536]{2,1,0:T(8,128)(2,1)S(1)}, u32[]{:S(2)}, u32[]{:S(2)}) collective-permute-start(bf16[2,64,1536]{2,1,0:T(8,128)(2,1)S(1)} %pad_maximum_fusion.2), channel_id=1, source_target_pairs={{2,0},{4,2},{6,4},{8,6},{10,8},{12,10},{14,12},{3,1},{5,3},{7,5},{... | collective-permute-start | bytes 1179656 | tf_op jit(solution)/shard_map/ppermute | solution.py:13
  445.3 0.9 copy-start.4
  445.3 1.0 copy-start.7
  446.4 0.9 copy-start.5
